TPU v7x, 32 devices: a whole 2x2x4 slice. The times are simulated.
32 devices in a mesh: pairs: 16 (over z, y, core), aux: 2 (over x).
Axes of the slice: x: 2, y: 2, z: 4, core: 2. Of those that a mesh axis runs over, the one named last changes fastest.
Arguments:
- amplitudes: float32 [64, 256, 256], P('pairs'), may hold values from -6 to 6
- factors: float32 [384, 256, 256], P('aux', 'pairs'), may hold values from -0.078125 to 0.078125
- occ_factors: float32 [384, 8, 8], P('aux'), may hold values from -0.5 to 0.5
Outputs:
- resid: float32 [64, 256, 256], P(None, 'pairs', 'aux')
All inputs are finite; a program needn't handle non-finite values.
Results may differ from a plain program's by a relative error of at most 0.0001.
Values sent between devices are 32-bit elements; how exact they have to be, the bound alone decides.
No kernel may reach another device: no remote copies, remote signals or barrier semaphores. Data moves between devices by JAX's collectives and lax.ppermute only.
A program may use at most 128 MiB of HBM per device.

v0:
```python
import jax
import jax.numpy as jnp
from jax import lax
from jax.sharding import PartitionSpec as P

highest = lax.Precision.HIGHEST


def from_partner(value, axis, bit):
    mask = 2**bit
    pairs = [(source, source ^ mask) for source in range(lax.axis_size(axis))]
    return lax.ppermute(value, axis, pairs)


def both_sides(running, amps, row_block):
    mixed_terms = jnp.einsum("icd,pbd->picb", amps, row_block, precision=highest)
    return running + jnp.einsum("pac,picb->iab", row_block, mixed_terms, precision=highest)


def shards(amplitudes, factors, occ_factors):
    virt_width = amplitudes.shape[1]
    aux_local = factors.shape[0]
    local_rows = factors.shape[1]
    occupied = occ_factors.shape[1]
    total_pairs = occupied * occupied
    aux_rank = lax.axis_index("aux")
    column_count = virt_width // lax.axis_size("aux")
    col_start = aux_rank * column_count
    amp_cols = lax.dynamic_slice_in_dim(amplitudes, col_start, column_count, 2)
    amp_flip = jnp.swapaxes(lax.dynamic_slice_in_dim(amplitudes, col_start, column_count, 1), 1, 2)
    pairs_rank = lax.axis_index("pairs")
    pairs_count = lax.axis_size("pairs")
    quarter_rows = aux_local // 4
    quarters = factors.reshape(1, 4, quarter_rows, local_rows, virt_width)
    outgoing = jnp.tile(quarters, (pairs_count // 4, 1, 1, 1, 1)).reshape(
        pairs_count, quarter_rows, local_rows, virt_width
    )
    arrived = lax.all_to_all(outgoing, "pairs", split_axis=0, concat_axis=2, tiled=True)[0]
    group_amps = amplitudes
    for bit in range(2):
        mate = from_partner(group_amps, "pairs", bit)
        lower = pairs_rank // 2**bit % 2 == 0
        group_amps = jnp.where(
            lower, jnp.concatenate([group_amps, mate], 0), jnp.concatenate([mate, group_amps], 0)
        )

    def quarter_step(running, block_index):
        row_block = lax.dynamic_slice_in_dim(arrived, block_index * 2, 2, 0)
        return (both_sides(running, group_amps, row_block), None)

    group_part, unused = lax.scan(
        quarter_step, jnp.zeros(group_amps.shape, jnp.float32), jnp.arange(quarter_rows // 2)
    )
    for bit in (1, 0):
        half = group_part.shape[0] // 2
        lower = pairs_rank // 2**bit % 2 == 0
        keep = jnp.where(lower, group_part[:half], group_part[half:])
        sending = jnp.where(lower, group_part[half:], group_part[:half])
        group_part = keep + from_partner(sending, "pairs", bit)
    particle = group_part
    coupling = jnp.einsum("pik,pjl->ijkl", occ_factors, occ_factors, precision=highest).reshape(
        total_pairs, total_pairs
    )
    particle, coupling = lax.psum((particle, coupling), "aux")
    part_cols = lax.dynamic_slice_in_dim(particle, col_start, column_count, 2)
    part_flip = jnp.swapaxes(lax.dynamic_slice_in_dim(particle, col_start, column_count, 1), 1, 2)
    part_cols, part_flip, amp_cols, amp_flip = (
        lax.all_to_all(part_cols, "pairs", split_axis=1, concat_axis=0, tiled=True),
        lax.all_to_all(part_flip, "pairs", split_axis=1, concat_axis=0, tiled=True),
        lax.all_to_all(amp_cols, "pairs", split_axis=1, concat_axis=0, tiled=True),
        lax.all_to_all(amp_flip, "pairs", split_axis=1, concat_axis=0, tiled=True),
    )
    straight = part_cols + jnp.einsum("pk,kab->pab", coupling, amp_cols, precision=highest)
    turned = part_flip + jnp.einsum("pk,kab->pab", coupling, amp_flip, precision=highest)
    rows_here = turned.shape[1]
    turned = (
        turned.reshape(occupied, occupied, rows_here, column_count)
        .transpose(1, 0, 2, 3)
        .reshape(total_pairs, rows_here, column_count)
    )
    return straight + turned


def solution(mesh):
    placed = (P("pairs", None, None), P("aux", "pairs", None), P("aux", None, None))
    return jax.shard_map(
        shards, mesh=mesh, in_specs=placed, out_specs=P(None, "pairs", "aux"), check_vma=False
    )
```

profile of v0, /device:TPU:0, one launch (start us, length us, event | category | flops | bytes accessed | tf_op | source)
XLA Modules:
  0.0 1026.3 jit_solution(16674948247421829473)
XLA Ops:
  30.0 141.6 %collective-permute-done.1 = f32[8,256,256]{2,1,0:T(8,128)} collective-permute-done((f32[8,256,256]{2,1,0:T(8,128)S(1)}, f32[8,256,256]{2,1,0:T(8,128)}, u32[]{:S(2)}, u32[]{:S(2)}) %collective-permute-start.1) | collective-permute-done | bytes 2097184 | tf_op jit(solution)/shard_map/ppermute | solution.py:12
  176.3 69.7 %all-to-all-done = f32[16,48,16,256]{3,2,1,0:T(8,128)} async-done(((f32[16,48,16,256]{3,2,1,0:T(8,128)}), f32[16,48,16,256]{3,2,1,0:T(8,128)}, u32[]{:S(2)}, u32[]{:S(2)}) %all-to-all-start) | async-done | bytes 12582944 | tf_op jit(solution)/shard_map/all_to_all | solution.py:38
  246.0 11.4 %copy.49 = f32[16,48,16,256]{3,2,0,1:T(8,128)} copy(f32[16,48,16,256]{3,2,1,0:T(8,128)} %all-to-all-done) | data formatting | bytes 25165824 | tf_op jit(solution)/shard_map/all_to_all | solution.py:38
  257.3 560.0 %while.11 = (s32[]{:T(128)}, f32[16,256,256]{1,2,0:T(8,128)}, s32[24]{0:T(128)S(1)}, f32[48,256,256]{2,1,0:T(8,128)}, f32[16,256,256]{2,1,0:T(8,128)}, /*index=5*/s32[]{:T(128)}, s32[1]{0:T(128)}, s32[]{:T(128)}, s32[]{:T(128)}) while((s32[]{:T(128)}, f32[16,256,256]{1,2,0:T(8,128)}, s32[24]{0:T(128)S(1)}, ...), condition=%wide.region_1.2_spmd.clone, body=%wide.region_0.1_spmd.clone.sunk | while | flops 12886999040 | bytes 30408872 | solution.py:51
  292.2 11.3 %bitcast_add_fusion.2 = f32[16,256,256]{1,2,0:T(8,128)} fusion(f32[16,256,256]{1,2,0:T(8,128)} %get-tuple-element.102, f32[2,256,16,256]{3,1,0,2:T(8,128)} %fusion.29, pred[]{:T(512)S(6)} %compare.8, f32[48,256,256]{2,1,0:T(8,128)} %get-tuple-element.113, s32[]{:T(128)S(6)} %select_n.97), kind=kOutput, calls=%fused_computation.2.clone.1 | convolution fusion | flops 6444548096 | bytes 17301508 | tf_op jit(solution)/shard_map/while/body/eval_jaxpr/pac,picb->iab/dot_general | solution.py:17
  315.6 11.2 %bitcast_add_fusion.2 = f32[16,256,256]{1,2,0:T(8,128)} fusion(f32[16,256,256]{1,2,0:T(8,128)} %get-tuple-element.102, f32[2,256,16,256]{3,1,0,2:T(8,128)} %fusion.29, pred[]{:T(512)S(6)} %compare.8, f32[48,256,256]{2,1,0:T(8,128)} %get-tuple-element.113, s32[]{:T(128)S(6)} %select_n.97), kind=kOutput, calls=%fused_computation.2.clone.1 | convolution fusion | flops 6444548096 | bytes 17301508 | tf_op jit(solution)/shard_map/while/body/eval_jaxpr/pac,picb->iab/dot_general | solution.py:17
  338.9 11.2 %bitcast_add_fusion.2 = f32[16,256,256]{1,2,0:T(8,128)} fusion(f32[16,256,256]{1,2,0:T(8,128)} %get-tuple-element.102, f32[2,256,16,256]{3,1,0,2:T(8,128)} %fusion.29, pred[]{:T(512)S(6)} %compare.8, f32[48,256,256]{2,1,0:T(8,128)} %get-tuple-element.113, s32[]{:T(128)S(6)} %select_n.97), kind=kOutput, calls=%fused_computation.2.clone.1 | convolution fusion | flops 6444548096 | bytes 17301508 | tf_op jit(solution)/shard_map/while/body/eval_jaxpr/pac,picb->iab/dot_general | solution.py:17
  362.3 11.2 %bitcast_add_fusion.2 = f32[16,256,256]{1,2,0:T(8,128)} fusion(f32[16,256,256]{1,2,0:T(8,128)} %get-tuple-element.102, f32[2,256,16,256]{3,1,0,2:T(8,128)} %fusion.29, pred[]{:T(512)S(6)} %compare.8, f32[48,256,256]{2,1,0:T(8,128)} %get-tuple-element.113, s32[]{:T(128)S(6)} %select_n.97), kind=kOutput, calls=%fused_computation.2.clone.1 | convolution fusion | flops 6444548096 | bytes 17301508 | tf_op jit(solution)/shard_map/while/body/eval_jaxpr/pac,picb->iab/dot_general | solution.py:17
  385.6 11.2 %bitcast_add_fusion.2 = f32[16,256,256]{1,2,0:T(8,128)} fusion(f32[16,256,256]{1,2,0:T(8,128)} %get-tuple-element.102, f32[2,256,16,256]{3,1,0,2:T(8,128)} %fusion.29, pred[]{:T(512)S(6)} %compare.8, f32[48,256,256]{2,1,0:T(8,128)} %get-tuple-element.113, s32[]{:T(128)S(6)} %select_n.97), kind=kOutput, calls=%fused_computation.2.clone.1 | convolution fusion | flops 6444548096 | bytes 17301508 | tf_op jit(solution)/shard_map/while/body/eval_jaxpr/pac,picb->iab/dot_general | solution.py:17
  409.0 11.2 %bitcast_add_fusion.2 = f32[16,256,256]{1,2,0:T(8,128)} fusion(f32[16,256,256]{1,2,0:T(8,128)} %get-tuple-element.102, f32[2,256,16,256]{3,1,0,2:T(8,128)} %fusion.29, pred[]{:T(512)S(6)} %compare.8, f32[48,256,256]{2,1,0:T(8,128)} %get-tuple-element.113, s32[]{:T(128)S(6)} %select_n.97), kind=kOutput, calls=%fused_computation.2.clone.1 | convolution fusion | flops 6444548096 | bytes 17301508 | tf_op jit(solution)/shard_map/while/body/eval_jaxpr/pac,picb->iab/dot_general | solution.py:17
  432.3 11.2 %bitcast_add_fusion.2 = f32[16,256,256]{1,2,0:T(8,128)} fusion(f32[16,256,256]{1,2,0:T(8,128)} %get-tuple-element.102, f32[2,256,16,256]{3,1,0,2:T(8,128)} %fusion.29, pred[]{:T(512)S(6)} %compare.8, f32[48,256,256]{2,1,0:T(8,128)} %get-tuple-element.113, s32[]{:T(128)S(6)} %select_n.97), kind=kOutput, calls=%fused_computation.2.clone.1 | convolution fusion | flops 6444548096 | bytes 17301508 | tf_op jit(solution)/shard_map/while/body/eval_jaxpr/pac,picb->iab/dot_general | solution.py:17
  455.7 11.2 %bitcast_add_fusion.2 = f32[16,256,256]{1,2,0:T(8,128)} fusion(f32[16,256,256]{1,2,0:T(8,128)} %get-tuple-element.102, f32[2,256,16,256]{3,1,0,2:T(8,128)} %fusion.29, pred[]{:T(512)S(6)} %compare.8, f32[48,256,256]{2,1,0:T(8,128)} %get-tuple-element.113, s32[]{:T(128)S(6)} %select_n.97), kind=kOutput, calls=%fused_computation.2.clone.1 | convolution fusion | flops 6444548096 | bytes 17301508 | tf_op jit(solution)/shard_map/while/body/eval_jaxpr/pac,picb->iab/dot_general | solution.py:17
  479.0 11.2 %bitcast_add_fusion.2 = f32[16,256,256]{1,2,0:T(8,128)} fusion(f32[16,256,256]{1,2,0:T(8,128)} %get-tuple-element.102, f32[2,256,16,256]{3,1,0,2:T(8,128)} %fusion.29, pred[]{:T(512)S(6)} %compare.8, f32[48,256,256]{2,1,0:T(8,128)} %get-tuple-element.113, s32[]{:T(128)S(6)} %select_n.97), kind=kOutput, calls=%fused_computation.2.clone.1 | convolution fusion | flops 6444548096 | bytes 17301508 | tf_op jit(solution)/shard_map/while/body/eval_jaxpr/pac,picb->iab/dot_general | solution.py:17
  525.7 11.3 %bitcast_add_fusion.2 = f32[16,256,256]{1,2,0:T(8,128)} fusion(f32[16,256,256]{1,2,0:T(8,128)} %get-tuple-element.102, f32[2,256,16,256]{3,1,0,2:T(8,128)} %fusion.29, pred[]{:T(512)S(6)} %compare.8, f32[48,256,256]{2,1,0:T(8,128)} %get-tuple-element.113, s32[]{:T(128)S(6)} %select_n.97), kind=kOutput, calls=%fused_computation.2.clone.1 | convolution fusion | flops 6444548096 | bytes 17301508 | tf_op jit(solution)/shard_map/while/body/eval_jaxpr/pac,picb->iab/dot_general | solution.py:17
  619.2 11.3 %bitcast_add_fusion.2 = f32[16,256,256]{1,2,0:T(8,128)} fusion(f32[16,256,256]{1,2,0:T(8,128)} %get-tuple-element.102, f32[2,256,16,256]{3,1,0,2:T(8,128)} %fusion.29, pred[]{:T(512)S(6)} %compare.8, f32[48,256,256]{2,1,0:T(8,128)} %get-tuple-element.113, s32[]{:T(128)S(6)} %select_n.97), kind=kOutput, calls=%fused_computation.2.clone.1 | convolution fusion | flops 6444548096 | bytes 17301508 | tf_op jit(solution)/shard_map/while/body/eval_jaxpr/pac,picb->iab/dot_general | solution.py:17
  642.6 11.3 %bitcast_add_fusion.2 = f32[16,256,256]{1,2,0:T(8,128)} fusion(f32[16,256,256]{1,2,0:T(8,128)} %get-tuple-element.102, f32[2,256,16,256]{3,1,0,2:T(8,128)} %fusion.29, pred[]{:T(512)S(6)} %compare.8, f32[48,256,256]{2,1,0:T(8,128)} %get-tuple-element.113, s32[]{:T(128)S(6)} %select_n.97), kind=kOutput, calls=%fused_computation.2.clone.1 | convolution fusion | flops 6444548096 | bytes 17301508 | tf_op jit(solution)/shard_map/while/body/eval_jaxpr/pac,picb->iab/dot_general | solution.py:17
  666.0 11.2 %bitcast_add_fusion.2 = f32[16,256,256]{1,2,0:T(8,128)} fusion(f32[16,256,256]{1,2,0:T(8,128)} %get-tuple-element.102, f32[2,256,16,256]{3,1,0,2:T(8,128)} %fusion.29, pred[]{:T(512)S(6)} %compare.8, f32[48,256,256]{2,1,0:T(8,128)} %get-tuple-element.113, s32[]{:T(128)S(6)} %select_n.97), kind=kOutput, calls=%fused_computation.2.clone.1 | convolution fusion | flops 6444548096 | bytes 17301508 | tf_op jit(solution)/shard_map/while/body/eval_jaxpr/pac,picb->iab/dot_general | solution.py:17
  689.3 11.2 %bitcast_add_fusion.2 = f32[16,256,256]{1,2,0:T(8,128)} fusion(f32[16,256,256]{1,2,0:T(8,128)} %get-tuple-element.102, f32[2,256,16,256]{3,1,0,2:T(8,128)} %fusion.29, pred[]{:T(512)S(6)} %compare.8, f32[48,256,256]{2,1,0:T(8,128)} %get-tuple-element.113, s32[]{:T(128)S(6)} %select_n.97), kind=kOutput, calls=%fused_computation.2.clone.1 | convolution fusion | flops 6444548096 | bytes 17301508 | tf_op jit(solution)/shard_map/while/body/eval_jaxpr/pac,picb->iab/dot_general | solution.py:17
  712.7 11.2 %bitcast_add_fusion.2 = f32[16,256,256]{1,2,0:T(8,128)} fusion(f32[16,256,256]{1,2,0:T(8,128)} %get-tuple-element.102, f32[2,256,16,256]{3,1,0,2:T(8,128)} %fusion.29, pred[]{:T(512)S(6)} %compare.8, f32[48,256,256]{2,1,0:T(8,128)} %get-tuple-element.113, s32[]{:T(128)S(6)} %select_n.97), kind=kOutput, calls=%fused_computation.2.clone.1 | convolution fusion | flops 6444548096 | bytes 17301508 | tf_op jit(solution)/shard_map/while/body/eval_jaxpr/pac,picb->iab/dot_general | solution.py:17
  825.5 17.5 %collective-permute-start.2 = (f32[8,256,256]{2,0,1:T(8,128)S(1)}, f32[8,256,256]{2,0,1:T(8,128)S(1)}, u32[]{:S(2)}, u32[]{:S(2)}) collective-permute-start(f32[8,256,256]{2,0,1:T(8,128)S(1)} %slice_select_fusion), channel_id=1, source_target_pairs={{0,4},{2,6},{4,0},{6,2},{8,12},{10,14},{12,8},{14,10},{16,20},{18,... | collective-permute-start | bytes 6291464 | tf_op jit(solution)/shard_map/ppermute | solution.py:12
  843.0 46.1 %collective-permute-done.2 = f32[8,256,256]{2,0,1:T(8,128)S(1)} collective-permute-done((f32[8,256,256]{2,0,1:T(8,128)S(1)}, f32[8,256,256]{2,0,1:T(8,128)S(1)}, u32[]{:S(2)}, u32[]{:S(2)}) %collective-permute-start.2) | collective-permute-done | bytes 2097184 | tf_op jit(solution)/shard_map/ppermute | solution.py:12
  893.8 37.8 %all-to-all-start.4 = ((f32[4,256,128]{2,0,1:T(4,128)}), f32[4,256,128]{2,0,1:T(4,128)}, u32[]{:S(2)}, u32[]{:S(2)}) async-start(f32[4,256,128]{2,0,1:T(4,128)} %bitcast.89), calls=%async_computation.4 | async-start | bytes 1048576 | tf_op jit(solution)/shard_map/all_to_all | solution.py:71
  950.1 26.1 %all-reduce.2.cloned.1.call-done = f32[4,256,256]{2,0,1:T(4,128)} async-done(((f32[4,256,256]{2,0,1:T(4,128)}), f32[4,256,256]{2,0,1:T(4,128)}) %all-reduce.2.cloned.1.call-update) | async-done | bytes 1048592 | tf_op jit(solution)/shard_map/psum | solution.py:64
  985.8 12.4 %all-to-all-done.3 = f32[4,256,128]{2,0,1:T(4,128)S(1)} async-done(((f32[4,256,128]{2,0,1:T(4,128)}), f32[4,256,128]{2,0,1:T(4,128)S(1)}, u32[]{:S(2)}, u32[]{:S(2)}) %all-to-all-start.3) | async-done | bytes 524320 | tf_op jit(solution)/shard_map/all_to_all | solution.py:69
  (108 shorter events, 464.6 us)
Async XLA Ops:
  6.5 995.9 %copy-start = (f32[192,8,8]{0,2,1:T(8,128)S(1)}, f32[192,8,8]{0,2,1:T(8,128)}, u32[]{:S(2)}) copy-start(f32[192,8,8]{0,2,1:T(8,128)} %param.7) | copy-start | bytes 147460
  14.7 7.6 copy-start.2
  14.7 231.2 %all-to-all-start = ((f32[16,48,16,256]{3,2,1,0:T(8,128)}), f32[16,48,16,256]{3,2,1,0:T(8,128)}, u32[]{:S(2)}, u32[]{:S(2)}) async-start(f32[16,48,16,256]{3,2,1,0:T(8,128)} %bitcast.83), calls=%async_computation | async-start | bytes 25165824 | tf_op jit(solution)/shard_map/all_to_all | solution.py:38
  22.4 4.0 collective-permute-start
  28.3 143.3 %collective-permute-start.1 = (f32[8,256,256]{2,1,0:T(8,128)S(1)}, f32[8,256,256]{2,1,0:T(8,128)}, u32[]{:S(2)}, u32[]{:S(2)}) collective-permute-start(f32[8,256,256]{2,1,0:T(8,128)S(1)} %maximum_select_fusion.1), channel_id=1, source_target_pairs={{0,4},{2,6},{4,0},{6,2},{8,12},{10,14},{12,8},{14,10},{16,20},{18,... | collective-permute-start | bytes 6291464 | tf_op jit(solution)/shard_map/ppermute | solution.py:12
  822.8 66.3 %copy-start.1 = (f32[16,256,256]{2,0,1:T(8,128)S(1)}, f32[16,256,256]{2,0,1:T(8,128)}, u32[]{:S(2)}) copy-start(f32[16,256,256]{2,0,1:T(8,128)} %copy.50) | copy-start | bytes 12582916
  825.5 63.7 %collective-permute-start.2 = (f32[8,256,256]{2,0,1:T(8,128)S(1)}, f32[8,256,256]{2,0,1:T(8,128)S(1)}, u32[]{:S(2)}, u32[]{:S(2)}) collective-permute-start(f32[8,256,256]{2,0,1:T(8,128)S(1)} %slice_select_fusion), channel_id=1, source_target_pairs={{0,4},{2,6},{4,0},{6,2},{8,12},{10,14},{12,8},{14,10},{16,20},{18,... | collective-permute-start | bytes 6291464 | tf_op jit(solution)/shard_map/ppermute | solution.py:12
  890.8 41.1 %collective-permute-start.3 = (f32[4,256,256]{2,0,1:T(4,128)}, f32[4,256,256]{2,0,1:T(4,128)}, u32[]{:S(2)}, u32[]{:S(2)}) collective-permute-start(f32[4,256,256]{2,0,1:T(4,128)} %slice_select_fusion.1), channel_id=1, source_target_pairs={{0,2},{2,0},{4,6},{6,4},{8,10},{10,8},{12,14},{14,12},{16,18},{18,... | collective-permute-start | bytes 3145736 | tf_op jit(solution)/shard_map/ppermute | solution.py:12
  893.8 52.1 %all-to-all-start.4 = ((f32[4,256,128]{2,0,1:T(4,128)}), f32[4,256,128]{2,0,1:T(4,128)}, u32[]{:S(2)}, u32[]{:S(2)}) async-start(f32[4,256,128]{2,0,1:T(4,128)} %bitcast.89), calls=%async_computation.4 | async-start | bytes 1048576 | tf_op jit(solution)/shard_map/all_to_all | solution.py:71
  931.6 44.6 %all-reduce.2.cloned.1.call-start = ((), (), s32[]{:S(2)}) async-start(), calls=%async_computation.5 | async-start | bytes 2097152 | tf_op jit(solution)/shard_map/psum | solution.py:64
  945.9 32.4 %all-to-all-start.2 = ((f32[4,256,128]{2,0,1:T(4,128)}), f32[4,256,128]{2,0,1:T(4,128)S(1)}, u32[]{:S(2)}, u32[]{:S(2)}) async-start(f32[4,256,128]{2,0,1:T(4,128)} %copy.68), calls=%async_computation.2 | async-start | bytes 1048576 | tf_op jit(solution)/shard_map/all_to_all | solution.py:70
  978.3 19.9 %all-to-all-start.3 = ((f32[4,256,128]{2,0,1:T(4,128)}), f32[4,256,128]{2,0,1:T(4,128)S(1)}, u32[]{:S(2)}, u32[]{:S(2)}) async-start(f32[4,256,128]{2,0,1:T(4,128)} %copy.57), calls=%async_computation.3 | async-start | bytes 1048576 | tf_op jit(solution)/shard_map/all_to_all | solution.py:69
  998.2 18.4 %all-to-all-start.1 = ((f32[4,256,128]{2,0,1:T(4,128)}), f32[4,256,128]{2,0,1:T(4,128)S(1)}, u32[]{:S(2)}, u32[]{:S(2)}) async-start(f32[4,256,128]{2,0,1:T(4,128)} %constant_dynamic-slice_fusion.2), calls=%async_computation.1 | async-start | bytes 1048576 | tf_op jit(solution)/shard_map/all_to_all | solution.py:68
Sparse Core Ops, SparseCore 0:
  934.7 41.4 all-reduce.1
where the time goes:
time: 1030 us
  matrix products  529 us (51%)
  waiting for transfers between devices  314 us (30%)
  starting transfers between devices  79.3 us (8%)
  local copies, waits for them, and re-layouts  52.8 us (5%)
  loops' own time  16.9 us (2%)
  between operations  13.6 us (1%)
  other arithmetic  13.5 us (1%)
    dot_general x24, matrix products, both_sides(): jnp.einsum('pac,picb->iab', row_block, mixed_terms, precision=highest)  269 us
    dot_general x24, matrix products, both_sides(): jnp.einsum('icd,pbd->picb', amps, row_block, precision=highest)  258 us
    ppermute x4, waiting for transfers between devices, from_partner(): return lax.ppermute(value, axis, pairs)  191 us
    all_to_all x1, waiting for transfers between devices, shards(): lax.all_to_all(outgoing, 'pairs', split_axis=0, concat_axis=2, tiled=True)  69.7 us
    all_to_all x1, starting transfers between devices, shards(): lax.all_to_all(amp_flip, 'pairs', split_axis=1, concat_axis=0, tiled=True)  37.8 us
    psum x1, waiting for transfers between devices, shards(): particle, coupling = lax.psum((particle, coupling), 'aux')  26.1 us
  transfers between devices with their start and end apart: 10, of which 8 were waited for; matrix products, arithmetic and copies ran while one was open for 2% of the time, Pallas kernels for 0%

commit v1 on v0

--- a/solution.py
+++ b/solution.py
@@ -4,6 +4,22 @@
 from jax.sharding import PartitionSpec as P
 
 highest = lax.Precision.HIGHEST
+
+
+def swapped_with_each(x, axis, split, join):
+    ways, here = (lax.axis_size(axis), lax.axis_index(axis))
+    width = x.shape[split] // ways
+    lengths = list(x.shape)
+    lengths[split] = width
+    height = lengths[join]
+    lengths[join] = height * ways
+    full = jnp.zeros(lengths, x.dtype)
+    for mask in range(ways):
+        part = lax.dynamic_slice_in_dim(x, (here ^ mask) * width, width, axis=split)
+        if mask:
+            part = lax.ppermute(part, axis, [(d, d ^ mask) for d in range(ways)])
+        full = lax.dynamic_update_slice_in_dim(full, part, (here ^ mask) * height, axis=join)
+    return full
 
 
 def from_partner(value, axis, bit):
@@ -35,7 +51,7 @@
     outgoing = jnp.tile(quarters, (pairs_count // 4, 1, 1, 1, 1)).reshape(
         pairs_count, quarter_rows, local_rows, virt_width
     )
-    arrived = lax.all_to_all(outgoing, "pairs", split_axis=0, concat_axis=2, tiled=True)[0]
+    arrived = swapped_with_each(outgoing, "pairs", 0, 2)[0]
     group_amps = amplitudes
     for bit in range(2):
         mate = from_partner(group_amps, "pairs", bit)

time: 1030 us -> 1060 us (1.029)
  starting transfers between devices: 79.3 us -> 153 us
  waiting for transfers between devices: 314 us -> 250 us
  local copies, waits for them, and re-layouts: 52.8 us -> 75.4 us
    ppermute x0 -> x15, waiting for transfers between devices: none -> 150 us  [swapped_with_each(): part = lax.ppermute(part, axis, [(d, d ^ mask) for d in range(ways)])]
    ppermute x4, waiting for transfers between devices: 191 us -> 47.2 us  [from_partner(): return lax.ppermute(value, axis, pairs)]
    ppermute x0 -> x15, starting transfers between devices: none -> 72.1 us  [swapped_with_each(): part = lax.ppermute(part, axis, [(d, d ^ mask) for d in range(ways)])]
    all_to_all x1 -> x0, waiting for transfers between devices: 69.7 us -> none  [shards(): lax.all_to_all(outgoing, 'pairs', split_axis=0, concat_axis=2, tiled=True)]
    all_to_all x1, starting transfers between devices: 4.16 us -> 65.9 us  [shards(): lax.all_to_all(amp_cols, 'pairs', split_axis=1, concat_axis=0, tiled=True)]
    all_to_all x1, starting transfers between devices: 37.8 us -> 4.17 us  [shards(): lax.all_to_all(amp_flip, 'pairs', split_axis=1, concat_axis=0, tiled=True)]
    dynamic_update_slice x0 -> x16, local copies, waits for them, and re-layouts: none -> 22.1 us  [swapped_with_each(): lax.dynamic_update_slice_in_dim(full, part, (here ^ mask) * height, axis=...]
    ppermute x4, starting transfers between devices: 19.8 us -> 1.47 us  [from_partner(): return lax.ppermute(value, axis, pairs)]
  transfers between devices with their start and end apart: 10 -> 24, of which waited for: 8 -> 12; matrix products, arithmetic and copies ran while one was open for 2% -> 4% of each run, Pallas kernels for 0% -> 0%
where the time goes in v1:
time: 1060 us
  matrix products  532 us (50%)
  waiting for transfers between devices  250 us (24%)
  starting transfers between devices  153 us (14%)
  local copies, waits for them, and re-layouts  75.4 us (7%)
  loops' own time  16.4 us (2%)
  between operations  13.7 us (1%)
  other arithmetic  11.3 us (1%)
    dot_general x24, matrix products, both_sides(): jnp.einsum('pac,picb->iab', row_block, mixed_terms, precision=highest)  270 us
    dot_general x24, matrix products, both_sides(): jnp.einsum('icd,pbd->picb', amps, row_block, precision=highest)  260 us
    ppermute x15, waiting for transfers between devices, swapped_with_each(): part = lax.ppermute(part, axis, [(d, d ^ mask) for d in range(ways)])  150 us
    ppermute x15, starting transfers between devices, swapped_with_each(): part = lax.ppermute(part, axis, [(d, d ^ mask) for d in range(ways)])  72.1 us
    all_to_all x1, starting transfers between devices, shards(): lax.all_to_all(amp_cols, 'pairs', split_axis=1, concat_axis=0, tiled=True)  65.9 us
    ppermute x4, waiting for transfers between devices, from_partner(): return lax.ppermute(value, axis, pairs)  47.2 us
    psum x1, waiting for transfers between devices, shards(): particle, coupling = lax.psum((particle, coupling), 'aux')  26 us
    dynamic_update_slice x16, local copies, waits for them, and re-layouts, swapped_with_each(): lax.dynamic_update_slice_in_dim(full, part, (here ^ mask) * height, axis=...  22.1 us
  transfers between devices with their start and end apart: 24, of which 12 were waited for; matrix products, arithmetic and copies ran while one was open for 4% of the time, Pallas kernels for 0%

profile of v1, /device:TPU:0, one launch (start us, length us, event | category | flops | bytes accessed | tf_op | source)
XLA Modules:
  0.0 1060.5 jit_solution(7103931251090970261)
XLA Ops:
  48.6 12.6 %collective-permute-done.2 = f32[1,48,16,256]{3,2,1,0:T(8,128)} collective-permute-done((f32[1,48,16,256]{3,2,1,0:T(8,128)}, f32[1,48,16,256]{3,2,1,0:T(8,128)}, u32[]{:S(2)}, u32[]{:S(2)}) %collective-permute-start.2) | collective-permute-done | bytes 786464 | tf_op jit(solution)/shard_map/ppermute | solution.py:20
  70.5 44.9 %collective-permute-done.5 = f32[1,48,16,256]{3,2,1,0:T(8,128)S(1)} collective-permute-done((f32[1,48,16,256]{3,2,1,0:T(8,128)S(1)}, f32[1,48,16,256]{3,2,1,0:T(8,128)S(1)}, u32[]{:S(2)}, u32[]{:S(2)}) %collective-permute-start.5) | collective-permute-done | bytes 786464 | tf_op jit(solution)/shard_map/ppermute | solution.py:20
  116.4 14.7 %collective-permute-done.6 = f32[1,48,16,256]{3,2,1,0:T(8,128)S(1)} collective-permute-done((f32[1,48,16,256]{3,2,1,0:T(8,128)S(1)}, f32[1,48,16,256]{3,2,1,0:T(8,128)S(1)}, u32[]{:S(2)}, u32[]{:S(2)}) %collective-permute-start.6) | collective-permute-done | bytes 786464 | tf_op jit(solution)/shard_map/ppermute | solution.py:20
  135.3 51.3 %collective-permute-start.12 = (f32[1,48,16,256]{3,2,1,0:T(8,128)S(1)}, f32[1,48,16,256]{3,2,1,0:T(8,128)S(1)}, u32[]{:S(2)}, u32[]{:S(2)}) collective-permute-start(f32[1,48,16,256]{3,2,1,0:T(8,128)S(1)} %copy-done.2), channel_id=1, source_target_pairs={{0,26},{2,24},{4,30},{6,28},{8,18},{10,16},{12,22},{14,20},{16,10}... | collective-permute-start | bytes 2359304 | tf_op jit(solution)/shard_map/ppermute | solution.py:20
  187.6 30.4 %collective-permute-done.9 = f32[1,48,16,256]{3,2,1,0:T(8,128)S(1)} collective-permute-done((f32[1,48,16,256]{3,2,1,0:T(8,128)S(1)}, f32[1,48,16,256]{3,2,1,0:T(8,128)S(1)}, u32[]{:S(2)}, u32[]{:S(2)}) %collective-permute-start.9) | collective-permute-done | bytes 786464 | tf_op jit(solution)/shard_map/ppermute | solution.py:20
  222.8 28.8 %collective-permute-done.10 = f32[1,48,16,256]{3,2,1,0:T(8,128)S(1)} collective-permute-done((f32[1,48,16,256]{3,2,1,0:T(8,128)S(1)}, f32[1,48,16,256]{3,2,1,0:T(8,128)S(1)}, u32[]{:S(2)}, u32[]{:S(2)}) %collective-permute-start.10) | collective-permute-done | bytes 786464 | tf_op jit(solution)/shard_map/ppermute | solution.py:20
  258.8 15.1 %collective-permute-done.14 = f32[1,48,16,256]{3,2,1,0:T(8,128)S(1)} collective-permute-done((f32[1,48,16,256]{3,2,1,0:T(8,128)S(1)}, f32[1,48,16,256]{3,2,1,0:T(8,128)S(1)}, u32[]{:S(2)}, u32[]{:S(2)}) %collective-permute-start.14) | collective-permute-done | bytes 786464 | tf_op jit(solution)/shard_map/ppermute | solution.py:20
  277.2 562.4 %while.11 = (s32[]{:T(128)}, f32[16,256,256]{1,2,0:T(8,128)}, s32[24]{0:T(128)S(1)}, f32[48,256,256]{2,1,0:T(8,128)}, f32[16,256,256]{2,1,0:T(8,128)}, /*index=5*/s32[]{:T(128)}, s32[1]{0:T(128)}, s32[]{:T(128)}, s32[]{:T(128)}) while((s32[]{:T(128)}, f32[16,256,256]{1,2,0:T(8,128)}, s32[24]{0:T(128)S(1)}, ...), condition=%wide.region_1.2_spmd.clone, body=%wide.region_0.1_spmd.clone.sunk | while | flops 12886999040 | bytes 30408880 | solution.py:67
  312.2 11.3 %bitcast_add_fusion.2 = f32[16,256,256]{1,2,0:T(8,128)} fusion(f32[16,256,256]{1,2,0:T(8,128)} %get-tuple-element.117, f32[2,256,16,256]{3,1,0,2:T(8,128)} %fusion.29, pred[]{:T(512)S(6)} %compare.8, f32[48,256,256]{2,1,0:T(8,128)} %get-tuple-element.128, s32[]{:T(128)S(6)} %select_n.225), kind=kOutput, calls=%fused_computation.2.clone.1 | convolution fusion | flops 6444548096 | bytes 17301508 | tf_op jit(solution)/shard_map/while/body/eval_jaxpr/pac,picb->iab/dot_general | solution.py:33
  335.6 11.3 %bitcast_add_fusion.2 = f32[16,256,256]{1,2,0:T(8,128)} fusion(f32[16,256,256]{1,2,0:T(8,128)} %get-tuple-element.117, f32[2,256,16,256]{3,1,0,2:T(8,128)} %fusion.29, pred[]{:T(512)S(6)} %compare.8, f32[48,256,256]{2,1,0:T(8,128)} %get-tuple-element.128, s32[]{:T(128)S(6)} %select_n.225), kind=kOutput, calls=%fused_computation.2.clone.1 | convolution fusion | flops 6444548096 | bytes 17301508 | tf_op jit(solution)/shard_map/while/body/eval_jaxpr/pac,picb->iab/dot_general | solution.py:33
  382.6 11.3 %bitcast_add_fusion.2 = f32[16,256,256]{1,2,0:T(8,128)} fusion(f32[16,256,256]{1,2,0:T(8,128)} %get-tuple-element.117, f32[2,256,16,256]{3,1,0,2:T(8,128)} %fusion.29, pred[]{:T(512)S(6)} %compare.8, f32[48,256,256]{2,1,0:T(8,128)} %get-tuple-element.128, s32[]{:T(128)S(6)} %select_n.225), kind=kOutput, calls=%fused_computation.2.clone.1 | convolution fusion | flops 6444548096 | bytes 17301508 | tf_op jit(solution)/shard_map/while/body/eval_jaxpr/pac,picb->iab/dot_general | solution.py:33
  429.5 11.3 %bitcast_add_fusion.2 = f32[16,256,256]{1,2,0:T(8,128)} fusion(f32[16,256,256]{1,2,0:T(8,128)} %get-tuple-element.117, f32[2,256,16,256]{3,1,0,2:T(8,128)} %fusion.29, pred[]{:T(512)S(6)} %compare.8, f32[48,256,256]{2,1,0:T(8,128)} %get-tuple-element.128, s32[]{:T(128)S(6)} %select_n.225), kind=kOutput, calls=%fused_computation.2.clone.1 | convolution fusion | flops 6444548096 | bytes 17301508 | tf_op jit(solution)/shard_map/while/body/eval_jaxpr/pac,picb->iab/dot_general | solution.py:33
  476.4 11.3 %bitcast_add_fusion.2 = f32[16,256,256]{1,2,0:T(8,128)} fusion(f32[16,256,256]{1,2,0:T(8,128)} %get-tuple-element.117, f32[2,256,16,256]{3,1,0,2:T(8,128)} %fusion.29, pred[]{:T(512)S(6)} %compare.8, f32[48,256,256]{2,1,0:T(8,128)} %get-tuple-element.128, s32[]{:T(128)S(6)} %select_n.225), kind=kOutput, calls=%fused_computation.2.clone.1 | convolution fusion | flops 6444548096 | bytes 17301508 | tf_op jit(solution)/shard_map/while/body/eval_jaxpr/pac,picb->iab/dot_general | solution.py:33
  523.3 11.3 %bitcast_add_fusion.2 = f32[16,256,256]{1,2,0:T(8,128)} fusion(f32[16,256,256]{1,2,0:T(8,128)} %get-tuple-element.117, f32[2,256,16,256]{3,1,0,2:T(8,128)} %fusion.29, pred[]{:T(512)S(6)} %compare.8, f32[48,256,256]{2,1,0:T(8,128)} %get-tuple-element.128, s32[]{:T(128)S(6)} %select_n.225), kind=kOutput, calls=%fused_computation.2.clone.1 | convolution fusion | flops 6444548096 | bytes 17301508 | tf_op jit(solution)/shard_map/while/body/eval_jaxpr/pac,picb->iab/dot_general | solution.py:33
  570.2 11.3 %bitcast_add_fusion.2 = f32[16,256,256]{1,2,0:T(8,128)} fusion(f32[16,256,256]{1,2,0:T(8,128)} %get-tuple-element.117, f32[2,256,16,256]{3,1,0,2:T(8,128)} %fusion.29, pred[]{:T(512)S(6)} %compare.8, f32[48,256,256]{2,1,0:T(8,128)} %get-tuple-element.128, s32[]{:T(128)S(6)} %select_n.225), kind=kOutput, calls=%fused_computation.2.clone.1 | convolution fusion | flops 6444548096 | bytes 17301508 | tf_op jit(solution)/shard_map/while/body/eval_jaxpr/pac,picb->iab/dot_general | solution.py:33
  617.1 11.3 %bitcast_add_fusion.2 = f32[16,256,256]{1,2,0:T(8,128)} fusion(f32[16,256,256]{1,2,0:T(8,128)} %get-tuple-element.117, f32[2,256,16,256]{3,1,0,2:T(8,128)} %fusion.29, pred[]{:T(512)S(6)} %compare.8, f32[48,256,256]{2,1,0:T(8,128)} %get-tuple-element.128, s32[]{:T(128)S(6)} %select_n.225), kind=kOutput, calls=%fused_computation.2.clone.1 | convolution fusion | flops 6444548096 | bytes 17301508 | tf_op jit(solution)/shard_map/while/body/eval_jaxpr/pac,picb->iab/dot_general | solution.py:33
  664.0 11.3 %bitcast_add_fusion.2 = f32[16,256,256]{1,2,0:T(8,128)} fusion(f32[16,256,256]{1,2,0:T(8,128)} %get-tuple-element.117, f32[2,256,16,256]{3,1,0,2:T(8,128)} %fusion.29, pred[]{:T(512)S(6)} %compare.8, f32[48,256,256]{2,1,0:T(8,128)} %get-tuple-element.128, s32[]{:T(128)S(6)} %select_n.225), kind=kOutput, calls=%fused_computation.2.clone.1 | convolution fusion | flops 6444548096 | bytes 17301508 | tf_op jit(solution)/shard_map/while/body/eval_jaxpr/pac,picb->iab/dot_general | solution.py:33
  711.0 11.3 %bitcast_add_fusion.2 = f32[16,256,256]{1,2,0:T(8,128)} fusion(f32[16,256,256]{1,2,0:T(8,128)} %get-tuple-element.117, f32[2,256,16,256]{3,1,0,2:T(8,128)} %fusion.29, pred[]{:T(512)S(6)} %compare.8, f32[48,256,256]{2,1,0:T(8,128)} %get-tuple-element.128, s32[]{:T(128)S(6)} %select_n.225), kind=kOutput, calls=%fused_computation.2.clone.1 | convolution fusion | flops 6444548096 | bytes 17301508 | tf_op jit(solution)/shard_map/while/body/eval_jaxpr/pac,picb->iab/dot_general | solution.py:33
  757.9 11.3 %bitcast_add_fusion.2 = f32[16,256,256]{1,2,0:T(8,128)} fusion(f32[16,256,256]{1,2,0:T(8,128)} %get-tuple-element.117, f32[2,256,16,256]{3,1,0,2:T(8,128)} %fusion.29, pred[]{:T(512)S(6)} %compare.8, f32[48,256,256]{2,1,0:T(8,128)} %get-tuple-element.128, s32[]{:T(128)S(6)} %select_n.225), kind=kOutput, calls=%fused_computation.2.clone.1 | convolution fusion | flops 6444548096 | bytes 17301508 | tf_op jit(solution)/shard_map/while/body/eval_jaxpr/pac,picb->iab/dot_general | solution.py:33
  804.8 11.3 %bitcast_add_fusion.2 = f32[16,256,256]{1,2,0:T(8,128)} fusion(f32[16,256,256]{1,2,0:T(8,128)} %get-tuple-element.117, f32[2,256,16,256]{3,1,0,2:T(8,128)} %fusion.29, pred[]{:T(512)S(6)} %compare.8, f32[48,256,256]{2,1,0:T(8,128)} %get-tuple-element.128, s32[]{:T(128)S(6)} %select_n.225), kind=kOutput, calls=%fused_computation.2.clone.1 | convolution fusion | flops 6444548096 | bytes 17301508 | tf_op jit(solution)/shard_map/while/body/eval_jaxpr/pac,picb->iab/dot_general | solution.py:33
  848.1 47.2 %collective-permute-done.17 = f32[8,256,256]{2,0,1:T(8,128)S(1)} collective-permute-done((f32[8,256,256]{2,0,1:T(8,128)S(1)}, f32[8,256,256]{2,0,1:T(8,128)S(1)}, u32[]{:S(2)}, u32[]{:S(2)}) %collective-permute-start.17) | collective-permute-done | bytes 2097184 | tf_op jit(solution)/shard_map/ppermute | solution.py:28
  900.3 65.9 %all-to-all-start.1 = ((f32[4,256,128]{2,0,1:T(4,128)}), f32[4,256,128]{2,0,1:T(4,128)}, u32[]{:S(2)}, u32[]{:S(2)}) async-start(f32[4,256,128]{2,0,1:T(4,128)} %copy.49), calls=%async_computation.1 | async-start | bytes 1048576 | tf_op jit(solution)/shard_map/all_to_all | solution.py:86
  984.7 26.0 %all-reduce.2.cloned.1.call-done = f32[4,256,256]{2,0,1:T(4,128)} async-done(((f32[4,256,256]{2,0,1:T(4,128)}), f32[4,256,256]{2,0,1:T(4,128)}) %all-reduce.2.cloned.1.call-update) | async-done | bytes 1048592 | tf_op jit(solution)/shard_map/psum | solution.py:80
  1020.3 12.1 %all-to-all-done = f32[4,256,128]{2,0,1:T(4,128)S(1)} async-done(((f32[4,256,128]{2,0,1:T(4,128)}), f32[4,256,128]{2,0,1:T(4,128)S(1)}, u32[]{:S(2)}, u32[]{:S(2)}) %all-to-all-start) | async-done | bytes 524320 | tf_op jit(solution)/shard_map/all_to_all | solution.py:84
  (167 shorter events, 545.8 us)
Async XLA Ops:
  23.0 13.2 %collective-permute-start = (f32[1,48,16,256]{3,2,1,0:T(8,128)}, f32[1,48,16,256]{3,2,1,0:T(8,128)}, u32[]{:S(2)}, u32[]{:S(2)}) collective-permute-start(f32[1,48,16,256]{3,2,1,0:T(8,128)} %get-tuple-element.75), channel_id=1, source_target_pairs={{0,2},{2,0},{4,6},{6,4},{8,10},{10,8},{12,14},{14,12},{16,18},{18,... | collective-permute-start | bytes 2359304 | tf_op jit(solution)/shard_map/ppermute | solution.py:20
  23.6 21.3 %collective-permute-start.1 = (f32[1,48,16,256]{3,2,1,0:T(8,128)}, f32[1,48,16,256]{3,2,1,0:T(8,128)}, u32[]{:S(2)}, u32[]{:S(2)}) collective-permute-start(f32[1,48,16,256]{3,2,1,0:T(8,128)} %get-tuple-element.74), channel_id=1, source_target_pairs={{0,4},{2,6},{4,0},{6,2},{8,12},{10,14},{12,8},{14,10},{16,20},{18,... | collective-permute-start | bytes 2359304 | tf_op jit(solution)/shard_map/ppermute | solution.py:20
  26.1 35.0 %collective-permute-start.2 = (f32[1,48,16,256]{3,2,1,0:T(8,128)}, f32[1,48,16,256]{3,2,1,0:T(8,128)}, u32[]{:S(2)}, u32[]{:S(2)}) collective-permute-start(f32[1,48,16,256]{3,2,1,0:T(8,128)} %get-tuple-element.73), channel_id=1, source_target_pairs={{0,6},{2,4},{4,2},{6,0},{8,14},{10,12},{12,10},{14,8},{16,22},{18,... | collective-permute-start | bytes 2359304 | tf_op jit(solution)/shard_map/ppermute | solution.py:20
  26.2 39.6 %collective-permute-start.3 = (f32[1,48,16,256]{3,2,1,0:T(8,128)}, f32[1,48,16,256]{3,2,1,0:T(8,128)}, u32[]{:S(2)}, u32[]{:S(2)}) collective-permute-start(f32[1,48,16,256]{3,2,1,0:T(8,128)} %get-tuple-element.72), channel_id=1, source_target_pairs={{0,8},{2,10},{4,12},{6,14},{8,0},{10,2},{12,4},{14,6},{16,24},{18,... | collective-permute-start | bytes 2359304 | tf_op jit(solution)/shard_map/ppermute | solution.py:20
  28.0 40.3 %collective-permute-start.4 = (f32[1,48,16,256]{3,2,1,0:T(8,128)}, f32[1,48,16,256]{3,2,1,0:T(8,128)}, u32[]{:S(2)}, u32[]{:S(2)}) collective-permute-start(f32[1,48,16,256]{3,2,1,0:T(8,128)} %get-tuple-element.71), channel_id=1, source_target_pairs={{0,10},{2,8},{4,14},{6,12},{8,2},{10,0},{12,6},{14,4},{16,26},{18,... | collective-permute-start | bytes 2359304 | tf_op jit(solution)/shard_map/ppermute | solution.py:20
  36.2 79.2 %collective-permute-start.5 = (f32[1,48,16,256]{3,2,1,0:T(8,128)S(1)}, f32[1,48,16,256]{3,2,1,0:T(8,128)S(1)}, u32[]{:S(2)}, u32[]{:S(2)}) collective-permute-start(f32[1,48,16,256]{3,2,1,0:T(8,128)S(1)} %copy-done.9), channel_id=1, source_target_pairs={{0,12},{2,14},{4,8},{6,10},{8,4},{10,6},{12,0},{14,2},{16,28},{18,... | collective-permute-start | bytes 2359304 | tf_op jit(solution)/shard_map/ppermute | solution.py:20
  44.9 86.2 %collective-permute-start.6 = (f32[1,48,16,256]{3,2,1,0:T(8,128)S(1)}, f32[1,48,16,256]{3,2,1,0:T(8,128)S(1)}, u32[]{:S(2)}, u32[]{:S(2)}) collective-permute-start(f32[1,48,16,256]{3,2,1,0:T(8,128)S(1)} %copy-done.8), channel_id=1, source_target_pairs={{0,14},{2,12},{4,10},{6,8},{8,6},{10,4},{12,2},{14,0},{16,30},{18,... | collective-permute-start | bytes 2359304 | tf_op jit(solution)/shard_map/ppermute | solution.py:20
  61.2 72.7 %collective-permute-start.7 = (f32[1,48,16,256]{3,2,1,0:T(8,128)S(1)}, f32[1,48,16,256]{3,2,1,0:T(8,128)S(1)}, u32[]{:S(2)}, u32[]{:S(2)}) collective-permute-start(f32[1,48,16,256]{3,2,1,0:T(8,128)S(1)} %copy-done.7), channel_id=1, source_target_pairs={{0,16},{2,18},{4,20},{6,22},{8,24},{10,26},{12,28},{14,30},{16,0},... | collective-permute-start | bytes 2359304 | tf_op jit(solution)/shard_map/ppermute | solution.py:20
  65.8 66.3 %collective-permute-start.15 = (f32[4,256,256]{2,1,0:T(8,128)S(1)}, f32[4,256,256]{2,1,0:T(8,128)S(1)}, u32[]{:S(2)}, u32[]{:S(2)}) collective-permute-start(f32[4,256,256]{2,1,0:T(8,128)S(1)} %copy-done.1), channel_id=1, source_target_pairs={{0,2},{2,0},{4,6},{6,4},{8,10},{10,8},{12,14},{14,12},{16,18},{18,... | collective-permute-start | bytes 3145736 | tf_op jit(solution)/shard_map/ppermute | solution.py:28
  68.3 67.1 %collective-permute-start.8 = (f32[1,48,16,256]{3,2,1,0:T(8,128)S(1)}, f32[1,48,16,256]{3,2,1,0:T(8,128)S(1)}, u32[]{:S(2)}, u32[]{:S(2)}) collective-permute-start(f32[1,48,16,256]{3,2,1,0:T(8,128)S(1)} %copy-done.6), channel_id=1, source_target_pairs={{0,18},{2,16},{4,22},{6,20},{8,26},{10,24},{12,30},{14,28},{16,2},... | collective-permute-start | bytes 2359304 | tf_op jit(solution)/shard_map/ppermute | solution.py:20
  115.4 102.6 %collective-permute-start.9 = (f32[1,48,16,256]{3,2,1,0:T(8,128)S(1)}, f32[1,48,16,256]{3,2,1,0:T(8,128)S(1)}, u32[]{:S(2)}, u32[]{:S(2)}) collective-permute-start(f32[1,48,16,256]{3,2,1,0:T(8,128)S(1)} %copy-done.5), channel_id=1, source_target_pairs={{0,20},{2,22},{4,16},{6,18},{8,28},{10,30},{12,24},{14,26},{16,4},... | collective-permute-start | bytes 2359304 | tf_op jit(solution)/shard_map/ppermute | solution.py:20
  131.1 120.5 %collective-permute-start.10 = (f32[1,48,16,256]{3,2,1,0:T(8,128)S(1)}, f32[1,48,16,256]{3,2,1,0:T(8,128)S(1)}, u32[]{:S(2)}, u32[]{:S(2)}) collective-permute-start(f32[1,48,16,256]{3,2,1,0:T(8,128)S(1)} %copy-done.4), channel_id=1, source_target_pairs={{0,22},{2,20},{4,18},{6,16},{8,30},{10,28},{12,26},{14,24},{16,6},... | collective-permute-start | bytes 2359304 | tf_op jit(solution)/shard_map/ppermute | solution.py:20
  132.1 123.8 %collective-permute-start.11 = (f32[1,48,16,256]{3,2,1,0:T(8,128)S(1)}, f32[1,48,16,256]{3,2,1,0:T(8,128)S(1)}, u32[]{:S(2)}, u32[]{:S(2)}) collective-permute-start(f32[1,48,16,256]{3,2,1,0:T(8,128)S(1)} %copy-done.3), channel_id=1, source_target_pairs={{0,24},{2,26},{4,28},{6,30},{8,16},{10,18},{12,20},{14,22},{16,8},... | collective-permute-start | bytes 2359304 | tf_op jit(solution)/shard_map/ppermute | solution.py:20
  133.9 141.0 %collective-permute-start.16 = (f32[8,256,256]{2,1,0:T(8,128)S(1)}, f32[8,256,256]{2,1,0:T(8,128)S(1)}, u32[]{:S(2)}, u32[]{:S(2)}) collective-permute-start(f32[8,256,256]{2,1,0:T(8,128)S(1)} %maximum_select_fusion.1), channel_id=1, source_target_pairs={{0,4},{2,6},{4,0},{6,2},{8,12},{10,14},{12,8},{14,10},{16,20},{18,... | collective-permute-start | bytes 6291464 | tf_op jit(solution)/shard_map/ppermute | solution.py:28
  135.3 121.5 %collective-permute-start.12 = (f32[1,48,16,256]{3,2,1,0:T(8,128)S(1)}, f32[1,48,16,256]{3,2,1,0:T(8,128)S(1)}, u32[]{:S(2)}, u32[]{:S(2)}) collective-permute-start(f32[1,48,16,256]{3,2,1,0:T(8,128)S(1)} %copy-done.2), channel_id=1, source_target_pairs={{0,26},{2,24},{4,30},{6,28},{8,18},{10,16},{12,22},{14,20},{16,10}... | collective-permute-start | bytes 2359304 | tf_op jit(solution)/shard_map/ppermute | solution.py:20
  218.0 39.8 %collective-permute-start.13 = (f32[1,48,16,256]{3,2,1,0:T(8,128)S(1)}, f32[1,48,16,256]{3,2,1,0:T(8,128)S(1)}, u32[]{:S(2)}, u32[]{:S(2)}) collective-permute-start(f32[1,48,16,256]{3,2,1,0:T(8,128)S(1)} %get-tuple-element.62), channel_id=1, source_target_pairs={{0,28},{2,30},{4,24},{6,26},{8,20},{10,22},{12,16},{14,18},{16,12}... | collective-permute-start | bytes 2359304 | tf_op jit(solution)/shard_map/ppermute | solution.py:20
  251.6 22.3 %collective-permute-start.14 = (f32[1,48,16,256]{3,2,1,0:T(8,128)S(1)}, f32[1,48,16,256]{3,2,1,0:T(8,128)S(1)}, u32[]{:S(2)}, u32[]{:S(2)}) collective-permute-start(f32[1,48,16,256]{3,2,1,0:T(8,128)S(1)} %get-tuple-element.61), channel_id=1, source_target_pairs={{0,30},{2,28},{4,26},{6,24},{8,22},{10,20},{12,18},{14,16},{16,14}... | collective-permute-start | bytes 2359304 | tf_op jit(solution)/shard_map/ppermute | solution.py:20
  847.5 47.7 %collective-permute-start.17 = (f32[8,256,256]{2,0,1:T(8,128)S(1)}, f32[8,256,256]{2,0,1:T(8,128)S(1)}, u32[]{:S(2)}, u32[]{:S(2)}) collective-permute-start(f32[8,256,256]{2,0,1:T(8,128)S(1)} %slice_select_fusion), channel_id=1, source_target_pairs={{0,4},{2,6},{4,0},{6,2},{8,12},{10,14},{12,8},{14,10},{16,20},{18,... | collective-permute-start | bytes 6291464 | tf_op jit(solution)/shard_map/ppermute | solution.py:28
  899.1 67.2 %collective-permute-start.18 = (f32[4,256,256]{2,0,1:T(4,128)}, f32[4,256,256]{2,0,1:T(4,128)}, u32[]{:S(2)}, u32[]{:S(2)}) collective-permute-start(f32[4,256,256]{2,0,1:T(4,128)} %slice_select_fusion.1), channel_id=1, source_target_pairs={{0,2},{2,0},{4,6},{6,4},{8,10},{10,8},{12,14},{14,12},{16,18},{18,... | collective-permute-start | bytes 3145736 | tf_op jit(solution)/shard_map/ppermute | solution.py:28
  900.3 80.3 %all-to-all-start.1 = ((f32[4,256,128]{2,0,1:T(4,128)}), f32[4,256,128]{2,0,1:T(4,128)}, u32[]{:S(2)}, u32[]{:S(2)}) async-start(f32[4,256,128]{2,0,1:T(4,128)} %copy.49), calls=%async_computation.1 | async-start | bytes 1048576 | tf_op jit(solution)/shard_map/all_to_all | solution.py:86
  966.2 44.5 %all-reduce.2.cloned.1.call-start = ((), (), s32[]{:S(2)}) async-start(), calls=%async_computation.4 | async-start | bytes 2097152 | tf_op jit(solution)/shard_map/psum | solution.py:80
  980.5 32.0 %all-to-all-start.3 = ((f32[4,256,128]{2,0,1:T(4,128)}), f32[4,256,128]{2,0,1:T(4,128)S(1)}, u32[]{:S(2)}, u32[]{:S(2)}) async-start(f32[4,256,128]{2,0,1:T(4,128)} %bitcast.32), calls=%async_computation.3 | async-start | bytes 1048576 | tf_op jit(solution)/shard_map/all_to_all | solution.py:87
  1012.5 19.9 %all-to-all-start = ((f32[4,256,128]{2,0,1:T(4,128)}), f32[4,256,128]{2,0,1:T(4,128)S(1)}, u32[]{:S(2)}, u32[]{:S(2)}) async-start(f32[4,256,128]{2,0,1:T(4,128)} %constant_dynamic-slice_fusion.1), calls=%async_computation | async-start | bytes 1048576 | tf_op jit(solution)/shard_map/all_to_all | solution.py:84
  1032.4 18.4 %all-to-all-start.2 = ((f32[4,256,128]{2,0,1:T(4,128)}), f32[4,256,128]{2,0,1:T(4,128)S(1)}, u32[]{:S(2)}, u32[]{:S(2)}) async-start(f32[4,256,128]{2,0,1:T(4,128)} %copy.38), calls=%async_computation.2 | async-start | bytes 1048576 | tf_op jit(solution)/shard_map/all_to_all | solution.py:85
  (10 other events, 1573.2 us)
Sparse Core Ops, SparseCore 0:
  969.3 41.3 all-reduce.1
